TPU v7x, 128 devices: a whole 4x4x4 slice. The times are simulated.
128 devices in a mesh: blk: 8 (over z_lo, x), head: 16 (over y, z_hi, core).
Axes of the slice: x: 4, y: 4, z: 4 (z_hi: 2, z_lo: 2; z = z_hi * 2 + z_lo), core: 2. Of those that a mesh axis runs over, the one named last changes fastest.
Arguments:
- qkv: bfloat16 [32768, 6144], P(('blk', 'head')), may hold values from -12 to 12
Outputs:
- attended: bfloat16 [32768, 2048], P(('blk', 'head'))
All inputs are finite; a program needn't handle non-finite values.
Results may differ from a plain program's by a relative error of at most 0.0059.
Values may be sent and summed in bfloat16 or wider, within the bound.
A program may use at most 128 MiB of HBM per device.

v0:
```python
import jax
import jax.numpy as jnp
from jax import lax
from jax.sharding import PartitionSpec as P

HEAD_DIM = 64
BLOCK = 2048
BLK_DEV = 2


def attend(query, pair):
    keys = pair[:, 0]
    values = pair[:, 1]
    tile = min(512, BLOCK)
    scale = HEAD_DIM ** (-0.5)

    def one_tile(query_tile):
        scores = (
            jnp.einsum("qhd,khd->hqk", query_tile, keys, preferred_element_type=jnp.float32) * scale
        )
        row_max = jnp.max(scores, axis=-1)
        probs = jnp.exp(scores - row_max[..., None]).astype(jnp.bfloat16)
        total = jnp.sum(probs.astype(jnp.float32), axis=-1)
        weighted = jnp.einsum("hqk,khd->hqd", probs, values, preferred_element_type=jnp.float32)
        return (row_max, total, weighted)

    tiles = query.reshape(BLOCK // tile, tile, query.shape[1], query.shape[2])
    return lax.map(one_tile, tiles)


def combine(partials):
    overall = partials[0][0]
    for entry in partials[1:]:
        overall = jnp.maximum(overall, entry[0])
    numer = jnp.zeros_like(partials[0][2])
    denom = jnp.zeros_like(partials[0][1])
    for row_max, total, weighted in partials:
        factor = jnp.exp(row_max - overall)
        numer = numer + factor[..., None] * weighted
        denom = denom + factor * total
    result = numer / denom[..., None]
    return result.transpose(0, 2, 1, 3).reshape(BLOCK, result.shape[1] * result.shape[3])


def on_device(qkv):
    rows = qkv.shape[0]
    heads_cols = qkv.shape[1] // 3
    shaped = qkv.reshape(rows, 3, heads_cols)
    grouped = lax.all_to_all(shaped, "head", split_axis=2, concat_axis=0, tiled=True)
    local_cols = grouped.shape[2]
    heads_here = local_cols // HEAD_DIM
    grid = grouped.reshape(BLK_DEV, BLOCK, 3, heads_here, HEAD_DIM)
    queries = grid[:, :, 0]
    pairs = grid[:, :, 1:3]
    device_bits = lax.axis_size("blk").bit_length() - 1
    partials = [[] for j in range(BLK_DEV)]

    def own_blocks():
        for j in range(BLK_DEV):
            partials[j].append(attend(queries[j], pairs[j]))
            partials[j].append(attend(queries[j], pairs[j ^ 1 << 0]))

    gathered = lax.all_gather(pairs, "blk", axis=0, tiled=True)
    mine = lax.axis_index("blk")
    for bit in range(device_bits):
        for j in range(BLK_DEV):
            where = jnp.bitwise_xor(mine, 1 << bit) * BLK_DEV + j
            chosen = lax.dynamic_index_in_dim(gathered, where, 0, keepdims=False)
            partials[j].append(attend(queries[j], chosen))
    own_blocks()
    outputs = jnp.concatenate([combine(partials[j]) for j in range(BLK_DEV)], axis=0).astype(
        jnp.bfloat16
    )
    return lax.all_to_all(outputs, "head", split_axis=0, concat_axis=1, tiled=True)


def solution(mesh):
    in_specs = (P(("blk", "head"), None),)
    out_specs = P(("blk", "head"), None)
    return jax.shard_map(
        on_device, mesh=mesh, in_specs=in_specs, out_specs=out_specs, check_vma=False
    )
```

profile of v0, /device:TPU:1, one launch (start us, length us, event | category | flops | bytes accessed | tf_op | source)
XLA Modules:
  0.0 471.0 jit_solution(7720879860149030022)
XLA Ops:
  6.5 3.2 copy.39
  9.7 17.2 %copy.40 = bf16[256,3,2048]{0,1,2:T(4,128)(2,1)} copy(bf16[256,3,2048]{0,2,1:T(8,128)(2,1)S(1)} %bitcast.366) | data formatting | bytes 6291456 | tf_op jit(solution)/shard_map/reshape | solution.py:48
  26.9 9.3 %all-to-all-start = ((bf16[256,3,2048]{0,1,2:T(4,128)(2,1)}), bf16[256,3,2048]{0,1,2:T(4,128)(2,1)}, u32[]{:S(2)}, u32[]{:S(2)}) async-start(bf16[256,3,2048]{0,1,2:T(4,128)(2,1)} %copy.40), calls=%async_computation | async-start | bytes 8388608 | tf_op jit(solution)/shard_map/all_to_all | solution.py:49
  36.2 52.6 %all-to-all-done = bf16[256,3,2048]{0,1,2:T(4,128)(2,1)} async-done(((bf16[256,3,2048]{0,1,2:T(4,128)(2,1)}), bf16[256,3,2048]{0,1,2:T(4,128)(2,1)}, u32[]{:S(2)}, u32[]{:S(2)}) %all-to-all-start) | async-done | bytes 3145760 | tf_op jit(solution)/shard_map/all_to_all | solution.py:49
  88.9 2.6 copy.41
  91.5 3.5 copy.42
  95.0 3.9 reshape.47
  100.8 5.2 %slice_reduce_fusion.1 = (bf16[2048,2,64]{0,2,1:T(8,128)(2,1)}, bf16[2048,2,64]{0,2,1:T(8,128)(2,1)}) fusion(bf16[2,2048,3,2,64]{1,0,4,3,2:T(2,128)(2,1)S(1)} %reshape.47), kind=kLoop, calls=%fused_computation.121 | loop fusion | bytes 2097152 | tf_op jit(solution)/shard_map/slice | solution.py:69
  106.0 4.2 fusion.62
  114.7 2.9 copy_bitcast_fusion
  118.9 21.6 %while.143 = (s32[]{:T(128)}, f32[4,2,512]{2,1,0:T(2,128)S(1)}, f32[4,2,512]{2,1,0:T(2,128)S(1)}, f32[4,2,512,64]{2,3,1,0:T(8,128)}, bf16[4,512,2,64]{1,3,2,0:T(...) while((s32[]{:T(128)}, f32[4,2,512]{2,1,0:T(2,128)S(1)}, ...), condition=%wide.region_15.16_spmd, body=%wide.region_12.15_spmd.sunk | while | flops 557840384 | bytes 26640988 | solution.py:28
  121.9 2.4 fusion.124
  127.3 2.3 fusion.124
  132.7 2.4 fusion.124
  138.1 2.4 fusion.124
  141.7 21.9 %while.144 = (s32[]{:T(128)}, f32[4,2,512]{2,1,0:T(2,128)S(1)}, f32[4,2,512]{2,1,0:T(2,128)S(1)}, f32[4,2,512,64]{2,3,1,0:T(8,128)}, bf16[4,512,2,64]{1,3,2,0:T(...) while((s32[]{:T(128)}, f32[4,2,512]{2,1,0:T(2,128)S(1)}, ...), condition=%wide.region_19.20_spmd, body=%wide.region_16.19_spmd.sunk | while | flops 557840384 | bytes 26640988 | solution.py:28
  145.0 2.4 fusion.127
  150.4 2.4 fusion.127
  155.8 2.4 fusion.127
  161.2 2.4 fusion.127
  164.7 21.6 %while.148 = (s32[]{:T(128)}, f32[4,2,512]{2,1,0:T(2,128)S(1)}, f32[4,2,512]{2,1,0:T(2,128)S(1)}, f32[4,2,512,64]{2,3,1,0:T(8,128)}, bf16[4,512,2,64]{1,3,2,0:T(...) while((s32[]{:T(128)}, f32[4,2,512]{2,1,0:T(2,128)S(1)}, ...), condition=%wide.region_35.36_spmd, body=%wide.region_32.35_spmd.sunk | while | flops 557840384 | bytes 26640988 | solution.py:28
  167.8 2.3 fusion.139
  173.2 2.4 fusion.139
  178.6 2.4 fusion.139
  184.0 2.4 fusion.139
  186.9 19.9 %while.149 = (s32[]{:T(128)}, f32[4,2,512]{2,1,0:T(2,128)S(1)}, f32[4,2,512]{2,1,0:T(2,128)S(1)}, f32[4,2,512,64]{2,3,1,0:T(8,128)S(1)}, bf16[4,512,2,64]{1,3,2,...) while((s32[]{:T(128)}, f32[4,2,512]{2,1,0:T(2,128)S(1)}, ...), condition=%wide.region_39.40_spmd, body=%wide.region_36.39_spmd.sunk | while | flops 557840384 | bytes 26640480 | solution.py:28
  206.8 83.2 %all-gather.2.cloned.1.call-done = bf16[16,2048,2,2,64]{1,4,3,2,0:T(8,128)(2,1)} async-done(((bf16[2,2048,2,2,64]{1,4,3,2,0:T(8,128)(2,1)}), bf16[16,2048,2,2,64]{1,4,3,2,0:T(8,128)(2,1)}) %all-gather.2.cloned.1.call-update) | async-done | bytes 16777232 | tf_op jit(solution)/shard_map/all_gather | solution.py:63
  290.1 5.3 %dynamic-slice_bitcast_fusion.5 = (bf16[2048,2,2,64]{0,3,2,1:T(8,128)(2,1)S(1)}, bf16[2048,2,2,64]{0,3,2,1:T(8,128)(2,1)}, bf16[2048,2,2,64]{0,3,2,1:T(8,128)(2,...) fusion(bf16[16,2048,2,2,64]{1,4,3,2,0:T(8,128)(2,1)} %all-gather.2., ...), kind=kLoop, calls=%fused_computation.132 | loop fusion | bytes 12582936 | tf_op jit(solution)/shard_map/jit(dynamic_index_in_dim)/squeeze | solution.py:68
  296.9 22.0 %while.140 = (s32[]{:T(128)}, f32[4,2,512]{2,1,0:T(2,128)S(1)}, f32[4,2,512]{2,1,0:T(2,128)S(1)}, f32[4,2,512,64]{2,3,1,0:T(8,128)}, bf16[4,512,2,64]{1,3,2,0:T(...) while((s32[]{:T(128)}, f32[4,2,512]{2,1,0:T(2,128)S(1)}, ...), condition=%wide.region_3.4_spmd, body=%wide.region_0.3_spmd.sunk | while | flops 557840384 | bytes 26640988 | solution.py:28
  300.3 2.4 fusion.115
  305.7 2.4 fusion.115
  311.2 2.4 fusion.115
  316.6 2.4 fusion.115
  319.1 19.9 %while.141 = (s32[]{:T(128)}, f32[4,2,512]{2,1,0:T(2,128)S(1)}, f32[4,2,512]{2,1,0:T(2,128)S(1)}, f32[4,2,512,64]{2,3,1,0:T(8,128)S(1)}, bf16[4,512,2,64]{1,3,2,...) while((s32[]{:T(128)}, f32[4,2,512]{2,1,0:T(2,128)S(1)}, ...), condition=%wide.region_7.8_spmd, body=%wide.region_4.7_spmd.sunk | while | flops 557840384 | bytes 26640480 | solution.py:28
  342.8 21.6 %while.142 = (s32[]{:T(128)}, f32[4,2,512]{2,1,0:T(2,128)S(1)}, f32[4,2,512]{2,1,0:T(2,128)S(1)}, f32[4,2,512,64]{2,3,1,0:T(8,128)}, bf16[4,512,2,64]{1,3,2,0:T(...) while((s32[]{:T(128)}, f32[4,2,512]{2,1,0:T(2,128)S(1)}, ...), condition=%wide.region_11.12_spmd, body=%wide.region_8.11_spmd.sunk | while | flops 557840384 | bytes 26640988 | solution.py:28
  345.8 2.4 fusion.121
  351.2 2.4 fusion.121
  362.0 2.4 fusion.121
  364.4 3.2 fusion.60
  368.3 20.1 %while.145 = (s32[]{:T(128)}, f32[4,2,512]{2,1,0:T(2,128)S(1)}, f32[4,2,512]{2,1,0:T(2,128)S(1)}, f32[4,2,512,64]{2,3,1,0:T(8,128)S(1)}, bf16[4,512,2,64]{1,3,2,...) while((s32[]{:T(128)}, f32[4,2,512]{2,1,0:T(2,128)S(1)}, ...), condition=%wide.region_23.24_spmd, body=%wide.region_20.23_spmd.sunk | while | flops 557840384 | bytes 26640480 | solution.py:28
  392.2 21.6 %while.146 = (s32[]{:T(128)}, f32[4,2,512]{2,1,0:T(2,128)S(1)}, f32[4,2,512]{2,1,0:T(2,128)S(1)}, f32[4,2,512,64]{2,3,1,0:T(8,128)}, bf16[4,512,2,64]{1,3,2,0:T(...) while((s32[]{:T(128)}, f32[4,2,512]{2,1,0:T(2,128)S(1)}, ...), condition=%wide.region_27.28_spmd, body=%wide.region_24.27_spmd.sunk | while | flops 557840384 | bytes 26640988 | solution.py:28
  395.3 2.4 fusion.133
  400.7 2.4 fusion.133
  406.1 2.4 fusion.133
  411.5 2.4 fusion.133
  414.0 19.9 %while.147 = (s32[]{:T(128)}, f32[4,2,512]{2,1,0:T(2,128)S(1)}, f32[4,2,512]{2,1,0:T(2,128)S(1)}, f32[4,2,512,64]{2,3,1,0:T(8,128)S(1)}, bf16[4,512,2,64]{1,3,2,...) while((s32[]{:T(128)}, f32[4,2,512]{2,1,0:T(2,128)S(1)}, ...), condition=%wide.region_31.32_spmd, body=%wide.region_28.31_spmd.sunk | while | flops 557840384 | bytes 26640480 | solution.py:28
  434.0 2.9 fusion.61
  438.2 23.8 %all_to_all.31 = bf16[16,256,128]{2,1,0:T(8,128)(2,1)S(1)} all-to-all(bf16[16,256,128]{2,1,0:T(8,128)(2,1)S(1)} %bitcast.367), channel_id=1, replica_groups=mesh['blk'=8,'head'=16] {'head'}, dimensions={0} | all-to-all | bytes 2097152 | tf_op jit(solution)/shard_map/all_to_all | solution.py:74
  (228 shorter events, 178.0 us)
Async XLA Ops:
  26.9 62.0 %all-to-all-start = ((bf16[256,3,2048]{0,1,2:T(4,128)(2,1)}), bf16[256,3,2048]{0,1,2:T(4,128)(2,1)}, u32[]{:S(2)}, u32[]{:S(2)}) async-start(bf16[256,3,2048]{0,1,2:T(4,128)(2,1)} %copy.40), calls=%async_computation | async-start | bytes 8388608 | tf_op jit(solution)/shard_map/all_to_all | solution.py:49
  36.2 253.9 %all-gather.2.cloned.1.call-start = ((), (), s32[]{:S(2)}) async-start(), calls=%async_computation.2 | async-start | bytes 18874368 | tf_op jit(solution)/shard_map/all_gather | solution.py:63
  110.2 4.5 copy-start
  140.5 1.2 copy-start.4
  140.5 1.2 copy-start.6
  163.6 1.1 copy-start.8
  163.6 1.1 copy-start.10
  186.3 0.6 copy-start.12
  186.3 0.6 copy-start.14
  206.8 88.6 %copy-start.1 = (f32[4,2,512,64]{2,3,1,0:T(8,128)}, f32[4,2,512,64]{2,3,1,0:T(8,128)S(1)}, u32[]{:S(2)}) copy-start(f32[4,2,512,64]{2,3,1,0:T(8,128)S(1)} %get-tuple-element.419) | copy-start | bytes 3145732
  206.8 88.9 %copy-start.16 = (f32[4,2,512]{2,1,0:T(2,128)}, f32[4,2,512]{2,1,0:T(2,128)S(1)}, u32[]{:S(2)}) copy-start(f32[4,2,512]{2,1,0:T(2,128)S(1)} %get-tuple-element.414) | copy-start | bytes 49156
  206.8 88.9 %copy-start.18 = (f32[4,2,512]{2,1,0:T(2,128)}, f32[4,2,512]{2,1,0:T(2,128)S(1)}, u32[]{:S(2)}) copy-start(f32[4,2,512]{2,1,0:T(2,128)S(1)} %get-tuple-element.424) | copy-start | bytes 49156
  339.0 1.0 copy-start.2
  342.7 21.6 %copy-start.5 = (f32[4,2,512]{2,1,0:T(2,128)S(1)}, f32[4,2,512]{2,1,0:T(2,128)}, u32[]{:S(2)}) copy-start(f32[4,2,512]{2,1,0:T(2,128)} %copy-done.4) | copy-start | bytes 49156
  342.7 21.6 %copy-start.7 = (f32[4,2,512]{2,1,0:T(2,128)S(1)}, f32[4,2,512]{2,1,0:T(2,128)}, u32[]{:S(2)}) copy-start(f32[4,2,512]{2,1,0:T(2,128)} %copy-done.6) | copy-start | bytes 49156
  342.8 21.6 %copy-start.9 = (f32[4,2,512]{2,1,0:T(2,128)S(1)}, f32[4,2,512]{2,1,0:T(2,128)}, u32[]{:S(2)}) copy-start(f32[4,2,512]{2,1,0:T(2,128)} %copy-done.8) | copy-start | bytes 49156
  342.8 21.6 %copy-start.11 = (f32[4,2,512]{2,1,0:T(2,128)S(1)}, f32[4,2,512]{2,1,0:T(2,128)}, u32[]{:S(2)}) copy-start(f32[4,2,512]{2,1,0:T(2,128)} %copy-done.10) | copy-start | bytes 49156
  388.4 1.0 copy-start.3
  414.0 20.0 %copy-start.13 = (f32[4,2,512]{2,1,0:T(2,128)S(1)}, f32[4,2,512]{2,1,0:T(2,128)}, u32[]{:S(2)}) copy-start(f32[4,2,512]{2,1,0:T(2,128)} %copy-done.12) | copy-start | bytes 49156
  414.0 20.0 %copy-start.15 = (f32[4,2,512]{2,1,0:T(2,128)S(1)}, f32[4,2,512]{2,1,0:T(2,128)}, u32[]{:S(2)}) copy-start(f32[4,2,512]{2,1,0:T(2,128)} %copy-done.14) | copy-start | bytes 49156
  414.0 20.0 %copy-start.17 = (f32[4,2,512]{2,1,0:T(2,128)S(1)}, f32[4,2,512]{2,1,0:T(2,128)}, u32[]{:S(2)}) copy-start(f32[4,2,512]{2,1,0:T(2,128)} %copy-done.16) | copy-start | bytes 49156
  414.0 20.0 %copy-start.19 = (f32[4,2,512]{2,1,0:T(2,128)S(1)}, f32[4,2,512]{2,1,0:T(2,128)}, u32[]{:S(2)}) copy-start(f32[4,2,512]{2,1,0:T(2,128)} %copy-done.18) | copy-start | bytes 49156
Sparse Core Ops, SparseCore 0:
  112.6 177.4 all-gather.1
where the time goes:
time: 477 us; the launch traced here: 471 us
  matrix products  142 us (30%)
  waiting for transfers between devices  136 us (29%)
  local copies, waits for them, and re-layouts  72 us (15%)
  other arithmetic  71.9 us (15%)
  blocking collectives  23.8 us (5%)
  between operations  14.1 us (3%)
  starting transfers between devices  9.34 us (2%)
    dot_general x40, matrix products, one_tile(): jnp.einsum('hqk,khd->hqd', probs, values, preferred_element_type=jnp.floa...  87 us
    all_gather x1, waiting for transfers between devices, on_device(): gathered = lax.all_gather(pairs, 'blk', axis=0, tiled=True)  83.2 us
    reduce_sum x40, other arithmetic, one_tile(): total = jnp.sum(probs.astype(jnp.float32), axis=-1)  65.6 us
    dot_general x40, matrix products, one_tile(): jnp.einsum('qhd,khd->hqk', query_tile, keys, preferred_element_type=jnp.f...  55.4 us
    all_to_all x1, waiting for transfers between devices, on_device(): lax.all_to_all(shaped, 'head', split_axis=2, concat_axis=0, tiled=True)  52.6 us
    all_to_all x1, blocking collectives, on_device(): lax.all_to_all(outputs, 'head', split_axis=0, concat_axis=1, tiled=True)  23.8 us
    reshape x1, local copies, waits for them, and re-layouts, on_device(): shaped = qkv.reshape(rows, 3, heads_cols)  17.2 us
  transfers between devices with their start and end apart: 2, of which 2 were waited for; matrix products, arithmetic and copies ran while one was open for 20% of the time, Pallas kernels for 0%

commit v1 on v0

--- a/solution.py
+++ b/solution.py
@@ -46,7 +46,11 @@
     rows = qkv.shape[0]
     heads_cols = qkv.shape[1] // 3
     shaped = qkv.reshape(rows, 3, heads_cols)
-    grouped = lax.all_to_all(shaped, "head", split_axis=2, concat_axis=0, tiled=True)
+    _find_face = lambda row_data: jnp.concatenate(
+        lax.all_to_all(jnp.stack(jnp.split(row_data, lax.axis_size("head"), 2)), "head", 0, 0),
+        axis=0,
+    )
+    grouped = _find_face(shaped)
     local_cols = grouped.shape[2]
     heads_here = local_cols // HEAD_DIM
     grid = grouped.reshape(BLK_DEV, BLOCK, 3, heads_here, HEAD_DIM)

time: 477 us -> 450 us (0.943)
  waiting for transfers between devices: 136 us -> 119 us
  local copies, waits for them, and re-layouts: 72 us -> 63.9 us
    reshape x2 -> x0, local copies, waits for them, and re-layouts: 21.1 us -> none  [the longest x1 17.2 us: on_device(): shaped = qkv.reshape(rows, 3, heads_cols)]
    all_to_all x1, waiting for transfers between devices: 52.6 us -> 39.7 us  [on_device(): lax.all_to_all(jnp.stack(jnp.split(row_data, lax.axis_size('head'), 2)),...]
    unnamed x44 -> x61, local copies, waits for them, and re-layouts: 8.72 us -> 19.8 us
    another operation x30 -> x32, local copies, waits for them, and re-layouts: 7.37 us -> 12 us
  transfers between devices with their start and end apart: 2 -> 2, of which waited for: 2 -> 2; matrix products, arithmetic and copies ran while one was open for 20% -> 21% of each run, Pallas kernels for 0% -> 0%
where the time goes in v1:
time: 450 us; the launch traced here: 447 us
  matrix products  142 us (32%)
  waiting for transfers between devices  119 us (26%)
  other arithmetic  72 us (16%)
  local copies, waits for them, and re-layouts  63.9 us (14%)
  blocking collectives  23.8 us (5%)
  between operations  14.1 us (3%)
  starting transfers between devices  9.34 us (2%)
    dot_general x40, matrix products, one_tile(): jnp.einsum('hqk,khd->hqd', probs, values, preferred_element_type=jnp.floa...  87 us
    all_gather x1, waiting for transfers between devices, on_device(): gathered = lax.all_gather(pairs, 'blk', axis=0, tiled=True)  79.8 us
    reduce_sum x40, other arithmetic, one_tile(): total = jnp.sum(probs.astype(jnp.float32), axis=-1)  65.6 us
    dot_general x40, matrix products, one_tile(): jnp.einsum('qhd,khd->hqk', query_tile, keys, preferred_element_type=jnp.f...  55.4 us
    all_to_all x1, waiting for transfers between devices, on_device(): lax.all_to_all(jnp.stack(jnp.split(row_data, lax.axis_size('head'), 2)),...  39.7 us
    all_to_all x1, blocking collectives, on_device(): lax.all_to_all(outputs, 'head', split_axis=0, concat_axis=1, tiled=True)  23.8 us
    unnamed x61, local copies, waits for them, and re-layouts  19.8 us
    all_to_all x1, starting transfers between devices, on_device(): lax.all_to_all(jnp.stack(jnp.split(row_data, lax.axis_size('head'), 2)),...  9.3 us
  transfers between devices with their start and end apart: 2, of which 2 were waited for; matrix products, arithmetic and copies ran while one was open for 21% of the time, Pallas kernels for 0%

profile of v1, /device:TPU:1, one launch (start us, length us, event | category | flops | bytes accessed | tf_op | source)
XLA Modules:
  0.0 446.6 jit_solution(14690774674157875450)
XLA Ops:
  6.5 3.2 copy.39
  20.7 9.3 %all-to-all-start = ((bf16[16,256,3,128]{1,3,2,0:T(8,128)(2,1)}), bf16[16,256,3,128]{1,3,2,0:T(8,128)(2,1)S(1)}, u32[]{:S(2)}, u32[]{:S(2)}) async-start(bf16[16,256,3,128]{1,3,2,0:T(8,128)(2,1)} %fusion.62), calls=%async_computation | async-start | bytes 6291456 | tf_op jit(solution)/shard_map/all_to_all | solution.py:50
  30.1 39.7 %all-to-all-done = bf16[16,256,3,128]{1,3,2,0:T(8,128)(2,1)S(1)} async-done(((bf16[16,256,3,128]{1,3,2,0:T(8,128)(2,1)}), bf16[16,256,3,128]{1,3,2,0:T(8,128)(2,1)S(1)}, u32[]{:S(2)}, u32[]{:S(2)}) %all-to-all-start) | async-done | bytes 3145760 | tf_op jit(solution)/shard_map/all_to_all | solution.py:50
  69.8 3.4 copy.40
  73.2 3.9 reshape_reshape.3
  79.0 5.2 %slice_reduce_fusion.1 = (bf16[2048,2,64]{0,2,1:T(8,128)(2,1)}, bf16[2048,2,64]{0,2,1:T(8,128)(2,1)}) fusion(bf16[2,2048,3,2,64]{1,0,4,3,2:T(2,128)(2,1)S(1)} %reshape_reshape.3), kind=kLoop, calls=%fused_computation.121 | loop fusion | bytes 2097152 | tf_op jit(solution)/shard_map/slice | solution.py:73
  84.2 4.2 fusion.78
  88.4 2.2 copy.41
  92.9 2.9 copy_bitcast_fusion
  97.1 21.7 %while.143 = (s32[]{:T(128)}, f32[4,2,512]{2,1,0:T(2,128)S(1)}, f32[4,2,512]{2,1,0:T(2,128)S(1)}, f32[4,2,512,64]{2,3,1,0:T(8,128)}, bf16[4,512,2,64]{1,3,2,0:T(...) while((s32[]{:T(128)}, f32[4,2,512]{2,1,0:T(2,128)S(1)}, ...), condition=%wide.region_15.16_spmd, body=%wide.region_12.15_spmd.sunk | while | flops 557840384 | bytes 26640988 | solution.py:28
  100.1 2.4 fusion.140
  105.5 2.4 fusion.140
  110.9 2.4 fusion.140
  116.3 2.4 fusion.140
  119.9 21.9 %while.144 = (s32[]{:T(128)}, f32[4,2,512]{2,1,0:T(2,128)S(1)}, f32[4,2,512]{2,1,0:T(2,128)S(1)}, f32[4,2,512,64]{2,3,1,0:T(8,128)}, bf16[4,512,2,64]{1,3,2,0:T(...) while((s32[]{:T(128)}, f32[4,2,512]{2,1,0:T(2,128)S(1)}, ...), condition=%wide.region_19.20_spmd, body=%wide.region_16.19_spmd.sunk | while | flops 557840384 | bytes 26640988 | solution.py:28
  123.2 2.4 fusion.143
  128.6 2.4 fusion.143
  134.0 2.4 fusion.143
  139.4 2.4 fusion.143
  142.9 21.6 %while.148 = (s32[]{:T(128)}, f32[4,2,512]{2,1,0:T(2,128)S(1)}, f32[4,2,512]{2,1,0:T(2,128)S(1)}, f32[4,2,512,64]{2,3,1,0:T(8,128)}, bf16[4,512,2,64]{1,3,2,0:T(...) while((s32[]{:T(128)}, f32[4,2,512]{2,1,0:T(2,128)S(1)}, ...), condition=%wide.region_35.36_spmd, body=%wide.region_32.35_spmd.sunk | while | flops 557840384 | bytes 26640988 | solution.py:28
  145.9 2.4 fusion.155
  151.3 2.4 fusion.155
  156.7 2.4 fusion.155
  162.1 2.4 fusion.155
  165.1 19.9 %while.149 = (s32[]{:T(128)}, f32[4,2,512]{2,1,0:T(2,128)S(1)}, f32[4,2,512]{2,1,0:T(2,128)S(1)}, f32[4,2,512,64]{2,3,1,0:T(8,128)S(1)}, bf16[4,512,2,64]{1,3,2,...) while((s32[]{:T(128)}, f32[4,2,512]{2,1,0:T(2,128)S(1)}, ...), condition=%wide.region_39.40_spmd, body=%wide.region_36.39_spmd.sunk | while | flops 557840384 | bytes 26640480 | solution.py:28
  185.0 79.8 %all-gather.2.cloned.1.call-done = bf16[16,2048,2,2,64]{1,4,3,2,0:T(8,128)(2,1)} async-done(((bf16[2,2048,2,2,64]{1,4,3,2,0:T(8,128)(2,1)}), bf16[16,2048,2,2,64]{1,4,3,2,0:T(8,128)(2,1)}) %all-gather.2.cloned.1.call-update) | async-done | bytes 16777232 | tf_op jit(solution)/shard_map/all_gather | solution.py:67
  264.8 5.3 %dynamic-slice_bitcast_fusion.5 = (bf16[2048,2,2,64]{0,3,2,1:T(8,128)(2,1)S(1)}, bf16[2048,2,2,64]{0,3,2,1:T(8,128)(2,1)}, bf16[2048,2,2,64]{0,3,2,1:T(8,128)(2,...) fusion(bf16[16,2048,2,2,64]{1,4,3,2,0:T(8,128)(2,1)} %all-gather.2., ...), kind=kLoop, calls=%fused_computation.132 | loop fusion | bytes 12582936 | tf_op jit(solution)/shard_map/jit(dynamic_index_in_dim)/squeeze | solution.py:72
  271.5 22.0 %while.140 = (s32[]{:T(128)}, f32[4,2,512]{2,1,0:T(2,128)S(1)}, f32[4,2,512]{2,1,0:T(2,128)S(1)}, f32[4,2,512,64]{2,3,1,0:T(8,128)}, bf16[4,512,2,64]{1,3,2,0:T(...) while((s32[]{:T(128)}, f32[4,2,512]{2,1,0:T(2,128)S(1)}, ...), condition=%wide.region_3.4_spmd, body=%wide.region_0.3_spmd.sunk | while | flops 557840384 | bytes 26640988 | solution.py:28
  275.0 2.4 fusion.131
  280.4 2.4 fusion.131
  285.8 2.3 fusion.131
  291.2 2.3 fusion.131
  293.7 19.9 %while.141 = (s32[]{:T(128)}, f32[4,2,512]{2,1,0:T(2,128)S(1)}, f32[4,2,512]{2,1,0:T(2,128)S(1)}, f32[4,2,512,64]{2,3,1,0:T(8,128)S(1)}, bf16[4,512,2,64]{1,3,2,...) while((s32[]{:T(128)}, f32[4,2,512]{2,1,0:T(2,128)S(1)}, ...), condition=%wide.region_7.8_spmd, body=%wide.region_4.7_spmd.sunk | while | flops 557840384 | bytes 26640480 | solution.py:28
  317.4 21.6 %while.142 = (s32[]{:T(128)}, f32[4,2,512]{2,1,0:T(2,128)S(1)}, f32[4,2,512]{2,1,0:T(2,128)S(1)}, f32[4,2,512,64]{2,3,1,0:T(8,128)}, bf16[4,512,2,64]{1,3,2,0:T(...) while((s32[]{:T(128)}, f32[4,2,512]{2,1,0:T(2,128)S(1)}, ...), condition=%wide.region_11.12_spmd, body=%wide.region_8.11_spmd.sunk | while | flops 557840384 | bytes 26640988 | solution.py:28
  320.4 2.3 fusion.137
  325.8 2.4 fusion.137
  331.2 2.3 fusion.137
  336.6 2.3 fusion.137
  339.0 3.3 fusion.60
  343.8 20.1 %while.145 = (s32[]{:T(128)}, f32[4,2,512]{2,1,0:T(2,128)S(1)}, f32[4,2,512]{2,1,0:T(2,128)S(1)}, f32[4,2,512,64]{2,3,1,0:T(8,128)S(1)}, bf16[4,512,2,64]{1,3,2,...) while((s32[]{:T(128)}, f32[4,2,512]{2,1,0:T(2,128)S(1)}, ...), condition=%wide.region_23.24_spmd, body=%wide.region_20.23_spmd.sunk | while | flops 557840384 | bytes 26640480 | solution.py:28
  367.6 21.6 %while.146 = (s32[]{:T(128)}, f32[4,2,512]{2,1,0:T(2,128)S(1)}, f32[4,2,512]{2,1,0:T(2,128)S(1)}, f32[4,2,512,64]{2,3,1,0:T(8,128)}, bf16[4,512,2,64]{1,3,2,0:T(...) while((s32[]{:T(128)}, f32[4,2,512]{2,1,0:T(2,128)S(1)}, ...), condition=%wide.region_27.28_spmd, body=%wide.region_24.27_spmd.sunk | while | flops 557840384 | bytes 26640988 | solution.py:28
  370.7 2.4 fusion.149
  376.1 2.4 fusion.149
  381.5 2.3 fusion.149
  386.9 2.3 fusion.149
  389.5 19.9 %while.147 = (s32[]{:T(128)}, f32[4,2,512]{2,1,0:T(2,128)S(1)}, f32[4,2,512]{2,1,0:T(2,128)S(1)}, f32[4,2,512,64]{2,3,1,0:T(8,128)S(1)}, bf16[4,512,2,64]{1,3,2,...) while((s32[]{:T(128)}, f32[4,2,512]{2,1,0:T(2,128)S(1)}, ...), condition=%wide.region_31.32_spmd, body=%wide.region_28.31_spmd.sunk | while | flops 557840384 | bytes 26640480 | solution.py:28
  409.5 3.0 fusion.61
  413.7 23.8 %all_to_all.21 = bf16[16,256,128]{2,1,0:T(8,128)(2,1)S(1)} all-to-all(bf16[16,256,128]{2,1,0:T(8,128)(2,1)S(1)} %bitcast.442), channel_id=1, replica_groups=mesh['blk'=8,'head'=16] {'head'}, dimensions={0} | all-to-all | bytes 2097152 | tf_op jit(solution)/shard_map/all_to_all | solution.py:78
  (244 shorter events, 185.2 us)
Async XLA Ops:
  20.7 49.1 %all-to-all-start = ((bf16[16,256,3,128]{1,3,2,0:T(8,128)(2,1)}), bf16[16,256,3,128]{1,3,2,0:T(8,128)(2,1)S(1)}, u32[]{:S(2)}, u32[]{:S(2)}) async-start(bf16[16,256,3,128]{1,3,2,0:T(8,128)(2,1)} %fusion.62), calls=%async_computation | async-start | bytes 6291456 | tf_op jit(solution)/shard_map/all_to_all | solution.py:50
  30.0 234.7 %all-gather.2.cloned.1.call-start = ((), (), s32[]{:S(2)}) async-start(), calls=%async_computation.2 | async-start | bytes 18874368 | tf_op jit(solution)/shard_map/all_gather | solution.py:67
  88.4 4.4 copy-start
  118.7 1.2 copy-start.5
  118.7 1.2 copy-start.7
  141.7 1.1 copy-start.9
  141.7 1.1 copy-start.11
  164.5 0.6 copy-start.13
  164.5 0.6 copy-start.15
  185.0 85.1 %copy-start.1 = (f32[4,2,512,64]{2,3,1,0:T(8,128)}, f32[4,2,512,64]{2,3,1,0:T(8,128)S(1)}, u32[]{:S(2)}) copy-start(f32[4,2,512,64]{2,3,1,0:T(8,128)S(1)} %get-tuple-element.419) | copy-start | bytes 3145732
  185.0 85.3 %copy-start.17 = (f32[4,2,512]{2,1,0:T(2,128)}, f32[4,2,512]{2,1,0:T(2,128)S(1)}, u32[]{:S(2)}) copy-start(f32[4,2,512]{2,1,0:T(2,128)S(1)} %get-tuple-element.414) | copy-start | bytes 49156
  185.0 85.3 %copy-start.19 = (f32[4,2,512]{2,1,0:T(2,128)}, f32[4,2,512]{2,1,0:T(2,128)S(1)}, u32[]{:S(2)}) copy-start(f32[4,2,512]{2,1,0:T(2,128)S(1)} %get-tuple-element.424) | copy-start | bytes 49156
  313.6 1.0 copy-start.2
  317.4 21.6 %copy-start.6 = (f32[4,2,512]{2,1,0:T(2,128)S(1)}, f32[4,2,512]{2,1,0:T(2,128)}, u32[]{:S(2)}) copy-start(f32[4,2,512]{2,1,0:T(2,128)} %copy-done.5) | copy-start | bytes 49156
  317.4 21.6 %copy-start.8 = (f32[4,2,512]{2,1,0:T(2,128)S(1)}, f32[4,2,512]{2,1,0:T(2,128)}, u32[]{:S(2)}) copy-start(f32[4,2,512]{2,1,0:T(2,128)} %copy-done.7) | copy-start | bytes 49156
  317.4 21.6 %copy-start.10 = (f32[4,2,512]{2,1,0:T(2,128)S(1)}, f32[4,2,512]{2,1,0:T(2,128)}, u32[]{:S(2)}) copy-start(f32[4,2,512]{2,1,0:T(2,128)} %copy-done.9) | copy-start | bytes 49156
  317.4 21.6 %copy-start.12 = (f32[4,2,512]{2,1,0:T(2,128)S(1)}, f32[4,2,512]{2,1,0:T(2,128)}, u32[]{:S(2)}) copy-start(f32[4,2,512]{2,1,0:T(2,128)} %copy-done.11) | copy-start | bytes 49156
  363.8 1.0 copy-start.3
  389.4 20.0 %copy-start.14 = (f32[4,2,512]{2,1,0:T(2,128)S(1)}, f32[4,2,512]{2,1,0:T(2,128)}, u32[]{:S(2)}) copy-start(f32[4,2,512]{2,1,0:T(2,128)} %copy-done.13) | copy-start | bytes 49156
  389.4 20.0 %copy-start.16 = (f32[4,2,512]{2,1,0:T(2,128)S(1)}, f32[4,2,512]{2,1,0:T(2,128)}, u32[]{:S(2)}) copy-start(f32[4,2,512]{2,1,0:T(2,128)} %copy-done.15) | copy-start | bytes 49156
  389.4 20.0 %copy-start.18 = (f32[4,2,512]{2,1,0:T(2,128)S(1)}, f32[4,2,512]{2,1,0:T(2,128)}, u32[]{:S(2)}) copy-start(f32[4,2,512]{2,1,0:T(2,128)} %copy-done.17) | copy-start | bytes 49156
  389.4 20.0 %copy-start.20 = (f32[4,2,512]{2,1,0:T(2,128)S(1)}, f32[4,2,512]{2,1,0:T(2,128)}, u32[]{:S(2)}) copy-start(f32[4,2,512]{2,1,0:T(2,128)} %copy-done.19) | copy-start | bytes 49156
  409.4 3.6 copy-start.4
Sparse Core Ops, SparseCore 0:
  90.8 173.9 all-gather.1
